TPU v7x, 256 devices: a whole 4x4x8 slice. The times are simulated.
256 devices in a mesh: seq: 16 (over y, x_lo, core), fsdp: 16 (over z, x_hi).
Axes of the slice: x: 4 (x_hi: 2, x_lo: 2; x = x_hi * 2 + x_lo), y: 4, z: 8, core: 2. Of those that a mesh axis runs over, the one named last changes fastest.
Arguments:
- clean_states: bfloat16 [16, 4096, 4096], P('fsdp', 'seq'), may hold values from -6 to 6
- noise_mask: int32 [16, 4096], P('fsdp', 'seq'), may hold values from 0 to 1, as said below
- mask_embed: bfloat16 [4096], replicated, may hold values from -6 to 6
- queries: bfloat16 [16, 4096, 2048], P('fsdp', 'seq'), may hold values from -96 to 96
- w_key: bfloat16 [4096, 512], P('fsdp'), may hold values from -0.09375 to 0.09375
- w_value: bfloat16 [4096, 512], P('fsdp'), may hold values from -0.09375 to 0.09375
Outputs:
- noisy_attention: bfloat16 [16, 4096, 2048], P('fsdp', 'seq')
Inputs may be any that keep to these rules, and one draw needn't show every extreme that they name: `noise_mask`: each block of 256 positions has its own masking rate; 1 marks a masked position.
All inputs are finite; a program needn't handle non-finite values.
Results may differ from a plain program's by a relative error of at most 0.011.
Values may be sent and summed in bfloat16 or wider, within the bound.
A program may use at most 64 MiB of HBM per device.

v0:
```python
import jax
import jax.numpy as jnp
from jax import lax
from jax.sharding import PartitionSpec as P

HEADS = 16
HEAD_DIM = 128
BLOCK = 256
ROPE_BASE = 500000.0


def rotate(key_rows, positions):
    half_dim = key_rows.shape[-1] // 2
    frequency = ROPE_BASE ** (-(jnp.arange(half_dim, dtype=jnp.float32) * 2.0 / key_rows.shape[-1]))
    angles = positions[:, None] * frequency[None, :]
    cosine = jnp.cos(angles)[:, None, :]
    sine_part = jnp.sin(angles)[:, None, :]
    first_half = key_rows[..., :half_dim]
    second_half = key_rows[..., half_dim:]
    return jnp.concatenate(
        [
            first_half * cosine - second_half * sine_part,
            second_half * cosine + first_half * sine_part,
        ],
        -1,
    )


def shards(clean_states, noise_mask, mask_embed, queries, w_key, w_value):
    states = clean_states[0]
    noise_marks = noise_mask[0]
    length_dev = states.shape[0]
    kv_width = w_key.shape[1]
    kv_count = kv_width // HEAD_DIM
    groups = HEADS // kv_count
    score_scale = HEAD_DIM ** (-0.5)
    query_rows = queries[0].reshape(length_dev, kv_count, groups, HEAD_DIM)
    source_rows = jnp.concatenate([states, mask_embed[None, :]], 0)
    pieces = (
        lax.all_gather(w_key, "fsdp", axis=0, tiled=True),
        lax.all_gather(w_value, "fsdp", axis=0, tiled=True),
    )
    key_all = jnp.dot(source_rows, pieces[0], preferred_element_type=jnp.float32)
    value_all = jnp.dot(source_rows, pieces[1], preferred_element_type=jnp.float32)
    masked_rows = noise_marks[:, None] == 1
    clean_key_sums = key_all[:length_dev]
    clean_value_sums = value_all[:length_dev]
    noisy_key_sums = jnp.where(masked_rows, key_all[length_dev:], clean_key_sums)
    noisy_value_sums = jnp.where(masked_rows, value_all[length_dev:], clean_value_sums)
    key_sums = jnp.concatenate([clean_key_sums, noisy_key_sums], 0)
    value_sums = jnp.concatenate([clean_value_sums, noisy_value_sums], 0)
    first_row = lax.axis_index("seq") * length_dev
    positions = first_row + jnp.arange(length_dev, dtype=jnp.int32)
    both_positions = jnp.concatenate([positions, positions]).astype(jnp.float32)
    key_rows = (
        rotate(key_sums.reshape(2 * length_dev, kv_count, HEAD_DIM), both_positions)
        .astype(jnp.bfloat16)
        .reshape(2 * length_dev, kv_width)
    )
    value_rows = value_sums.astype(jnp.bfloat16)
    clean_keys = key_rows[:length_dev]
    clean_values = value_rows[:length_dev]
    noisy_keys = key_rows[length_dev:]
    noisy_values = value_rows[length_dev:]
    query_block = positions // BLOCK

    def absorb(running, key_part, value_part, allowed):
        row_max, row_sum, mixture = running
        key_count = key_part.shape[0]
        scores = (
            jnp.einsum(
                "qkgd,tkd->qkgt",
                query_rows,
                key_part.reshape(key_count, kv_count, HEAD_DIM),
                preferred_element_type=jnp.float32,
            )
            * score_scale
        )
        mask_wide = allowed[:, None, None, :]
        scores = jnp.where(mask_wide, scores, -1e30)
        new_max = jnp.maximum(row_max, jnp.max(scores, -1))
        weights = jnp.where(mask_wide, jnp.exp(scores - new_max[..., None]), 0.0)
        rescale = jnp.exp(row_max - new_max)
        row_sum = row_sum * rescale + jnp.sum(weights, -1)
        mixture = mixture * rescale[..., None] + jnp.einsum(
            "qkgt,tkd->qkgd",
            weights.astype(jnp.bfloat16),
            value_part.reshape(key_count, kv_count, HEAD_DIM),
            preferred_element_type=jnp.float32,
        )
        return (new_max, row_sum, mixture)

    def sweep(running, key_stack, value_stack, start_row, same_copy):
        rounds = key_stack.shape[0] // BLOCK

        def sub_step(number, running):
            offset = number * BLOCK
            key_part = lax.dynamic_slice_in_dim(key_stack, offset, BLOCK, 0)
            value_part = lax.dynamic_slice_in_dim(value_stack, offset, BLOCK, 0)
            key_block = (start_row + offset) // BLOCK
            if same_copy:
                allowed = query_block[:, None] == key_block
            else:
                allowed = (query_block[:, None] > key_block) & (key_block >= 0)
            allowed = jnp.broadcast_to(allowed, (length_dev, BLOCK))
            return absorb(running, key_part, value_part, allowed)

        return lax.fori_loop(0, rounds, sub_step, running)

    running = (
        jnp.full((length_dev, kv_count, groups), -1e30, jnp.float32),
        jnp.zeros((length_dev, kv_count, groups), jnp.float32),
        jnp.zeros((length_dev, kv_count, groups, HEAD_DIM), jnp.float32),
    )
    running = sweep(running, noisy_keys, noisy_values, first_row, True)
    pieces = (
        lax.all_gather(clean_keys, "seq", axis=0, tiled=True),
        lax.all_gather(clean_values, "seq", axis=0, tiled=True),
    )
    running = sweep(running, pieces[0], pieces[1], jnp.int32(0), False)
    row_max, row_sum, mixture = running
    output = (
        (mixture / row_sum[..., None])
        .astype(jnp.bfloat16)
        .reshape(length_dev, kv_count * groups * HEAD_DIM)
    )
    return output[None]


def solution(mesh):
    placed = (
        P("fsdp", "seq", None),
        P("fsdp", "seq"),
        P(),
        P("fsdp", "seq", None),
        P("fsdp", None),
        P("fsdp", None),
    )
    return jax.shard_map(
        shards, mesh=mesh, in_specs=placed, out_specs=P("fsdp", "seq", None), check_vma=False
    )
```

profile of v0, /device:TPU:1, one launch (start us, length us, event | category | flops | bytes accessed | tf_op | source)
XLA Modules:
  0.0 420.3 jit_solution(12876547095858596038)
XLA Ops:
  9.5 101.1 %all-gather.7.cloned.1.call-done = bf16[4096,512]{1,0:T(8,128)(2,1)} async-done(((bf16[256,512]{1,0:T(8,128)(2,1)}), bf16[4096,512]{1,0:T(8,128)(2,1)}) %all-gather.7.cloned.1.call-update) | async-done | bytes 4194320 | tf_op jit(solution)/shard_map/all_gather | solution.py:41
  110.5 4.2 %fusion.33 = f32[257,512]{1,0:T(8,128)S(1)} fusion(bf16[4096,512]{1,0:T(8,128)(2,1)} %all-gather.7.cloned.1.call-done, bf16[1,4096]{1,0:T(2,128)(2,1)S(1)} %broadcast_in_dim.141, bf16[256,4096]{1,0:T(8,128)(2,1)} %bitcast.118), kind=kOutput, calls=%fused_computation.45 | convolution fusion | flops 1082146816 | bytes 6825984 | tf_op jit(solution)/shard_map/dot_general | solution.py:44
  116.7 93.1 %all-gather.5.cloned.1.call-done = bf16[4096,512]{1,0:T(8,128)(2,1)} async-done(((bf16[256,512]{1,0:T(8,128)(2,1)}), bf16[4096,512]{1,0:T(8,128)(2,1)}) %all-gather.5.cloned.1.call-update) | async-done | bytes 4194320 | tf_op jit(solution)/shard_map/all_gather | solution.py:40
  209.7 3.5 fusion.34
  215.7 1.5 copy.18
  220.8 2.5 bitcast_add_fusion.1
  223.3 28.4 %all-gather.11.cloned.1.call-done = bf16[4096,512]{1,0:T(8,128)(2,1)} async-done(((bf16[256,512]{1,0:T(8,128)(2,1)}), bf16[4096,512]{1,0:T(8,128)(2,1)}) %all-gather.11.cloned.1.call-update) | async-done | bytes 4194320 | tf_op jit(solution)/shard_map/all_gather | solution.py:118
  251.7 50.2 %all-gather.9.cloned.1.call-done = bf16[4096,512]{0,1:T(8,128)(2,1)} async-done(((bf16[256,512]{0,1:T(8,128)(2,1)}), bf16[4096,512]{0,1:T(8,128)(2,1)}) %all-gather.9.cloned.1.call-update) | async-done | bytes 4194320 | tf_op jit(solution)/shard_map/all_gather | solution.py:117
  301.9 108.7 %while.13 = (s32[]{:T(128)}, f32[256,4,4]{0,2,1:T(4,128)S(1)}, f32[256,4,4]{0,2,1:T(4,128)S(1)}, f32[256,4,4,128]{0,3,2,1:T(8,128)}, bf16[4096,512]{0,1:T(8,128)...) while((s32[]{:T(128)}, f32[256,4,4]{0,2,1:T(4,128)S(1)}, ...), condition=%wide.region_5.6_spmd.clone, body=%wide.region_2.5_spmd.clone.sunk | while | flops 551563776 | bytes 36963736 | solution.py:108
  305.9 1.4 bitcast_add_fusion.3
  312.7 1.4 bitcast_add_fusion.3
  319.5 1.4 bitcast_add_fusion.3
  326.3 1.4 bitcast_add_fusion.3
  333.1 1.4 bitcast_add_fusion.3
  339.9 1.4 bitcast_add_fusion.3
  346.7 1.4 bitcast_add_fusion.3
  360.3 1.4 bitcast_add_fusion.3
  367.1 1.4 bitcast_add_fusion.3
  380.6 1.4 bitcast_add_fusion.3
  387.4 1.4 bitcast_add_fusion.3
  401.0 1.4 bitcast_add_fusion.3
  407.8 1.4 bitcast_add_fusion.3
  410.6 1.8 divide_convert_fusion
  412.4 1.4 copy.34
  (246 shorter events, 100.1 us)
Async XLA Ops:
  6.5 104.0 %all-gather.7.cloned.1.call-start = ((), (), s32[]{:S(2)}) async-start(), calls=%async_computation.1 | async-start | bytes 4456448 | tf_op jit(solution)/shard_map/all_gather | solution.py:41
  7.3 202.5 %all-gather.5.cloned.1.call-start = ((), (), s32[]{:S(2)}) async-start(), calls=%async_computation | async-start | bytes 4456448 | tf_op jit(solution)/shard_map/all_gather | solution.py:40
  8.0 243.7 %all-gather.11.cloned.1.call-start = ((), (), s32[]{:S(2)}) async-start(), calls=%async_computation.3 | async-start | bytes 4456448 | tf_op jit(solution)/shard_map/all_gather | solution.py:118
  110.5 99.2 %copy-start.3 = (bf16[1,256,4096]{2,1,0:T(8,128)(2,1)S(1)}, bf16[1,256,4096]{2,1,0:T(8,128)(2,1)}, u32[]{:S(2)}) copy-start(bf16[1,256,4096]{2,1,0:T(8,128)(2,1)} %param.8) | copy-start | bytes 6291460
  115.6 186.3 %all-gather.9.cloned.1.call-start = ((), (), s32[]{:S(2)}) async-start(), calls=%async_computation.2 | async-start | bytes 4456448 | tf_op jit(solution)/shard_map/all_gather | solution.py:117
  218.8 1.9 copy-start.2
  304.0 1.9 copy-start
  307.3 1.4 copy-start.1
  310.8 1.9 copy-start
  317.6 1.9 copy-start
  324.4 1.9 copy-start
  331.2 1.9 copy-start
  334.5 1.4 copy-start.1
  338.0 1.9 copy-start
  344.8 1.9 copy-start
  351.6 1.9 copy-start
  358.3 1.9 copy-start
  365.1 1.9 copy-start
  371.9 1.9 copy-start
  378.7 1.9 copy-start
  385.5 1.9 copy-start
  392.3 1.9 copy-start
  399.1 1.9 copy-start
  405.9 1.9 copy-start
  (14 other events, 19.2 us)
Sparse Core Ops, SparseCore 0:
  9.9 100.5 all-gather.6
  113.1 96.5 all-gather.4
  211.6 40.0 all-gather.10
  253.3 48.5 all-gather.8
where the time goes:
time: 422 us; the launch traced here: 420 us
  waiting for transfers between devices  274 us (65%)
  local copies, waits for them, and re-layouts  62 us (15%)
  matrix products  46.7 us (11%)
  other arithmetic  22.8 us (5%)
  between operations  13.3 us (3%)
    all_gather x1, waiting for transfers between devices, shards(): lax.all_gather(w_value, 'fsdp', axis=0, tiled=True)  101 us
    all_gather x1, waiting for transfers between devices, shards(): lax.all_gather(w_key, 'fsdp', axis=0, tiled=True)  93.1 us
    all_gather x1, waiting for transfers between devices, shards(): lax.all_gather(clean_keys, 'seq', axis=0, tiled=True)  50.2 us
    all_gather x1, waiting for transfers between devices, shards(): lax.all_gather(clean_values, 'seq', axis=0, tiled=True)  28.4 us
    dot_general x17, matrix products, absorb(): jnp.einsum('qkgt,tkd->qkgd', weights.astype(jnp.bfloat16), value_part.res...  24.7 us
    while x80, local copies, waits for them, and re-layouts  21.8 us
    dynamic_slice x32, local copies, waits for them, and re-layouts, sub_step(): value_part = lax.dynamic_slice_in_dim(value_stack, offset, BLOCK, 0)  17.7 us
    reduce_sum x17, other arithmetic, absorb(): row_sum = row_sum * rescale + jnp.sum(weights, -1)  17.4 us
  transfers between devices with their start and end apart: 4, of which 4 were waited for; matrix products, arithmetic and copies ran while one was open for 5% of the time, Pallas kernels for 0%

commit v1 on v0

--- a/solution.py
+++ b/solution.py
@@ -36,10 +36,14 @@
     score_scale = HEAD_DIM ** (-0.5)
     query_rows = queries[0].reshape(length_dev, kv_count, groups, HEAD_DIM)
     source_rows = jnp.concatenate([states, mask_embed[None, :]], 0)
-    pieces = (
-        lax.all_gather(w_key, "fsdp", axis=0, tiled=True),
-        lax.all_gather(w_value, "fsdp", axis=0, tiled=True),
-    )
+
+    def lead_page(chunk):
+        tile_out = jnp.stack(lax.axis_size("fsdp") * [chunk], 0)
+        y_new = lax.all_to_all(tile_out, "fsdp", 0, 0)
+        ready = jnp.concatenate(y_new, 0)
+        return ready
+
+    pieces = (lax.all_gather(w_key, "fsdp", axis=0, tiled=True), lead_page(w_value))
     key_all = jnp.dot(source_rows, pieces[0], preferred_element_type=jnp.float32)
     value_all = jnp.dot(source_rows, pieces[1], preferred_element_type=jnp.float32)
     masked_rows = noise_marks[:, None] == 1

time: 422 us -> 382 us (0.905)
  waiting for transfers between devices: 274 us -> 221 us
  starting transfers between devices: 0.12 us -> 12 us
    all_gather x1 -> x0, waiting for transfers between devices: 101 us -> none  [shards(): lax.all_gather(w_value, 'fsdp', axis=0, tiled=True)]
    all_gather x1, waiting for transfers between devices: 93.1 us -> 143 us  [shards(): lax.all_gather(w_key, 'fsdp', axis=0, tiled=True)]
    all_gather x1, waiting for transfers between devices: 50.2 us -> 36.6 us  [shards(): lax.all_gather(clean_keys, 'seq', axis=0, tiled=True)]
    all_gather x1, waiting for transfers between devices: 28.4 us -> 41.1 us  [shards(): lax.all_gather(clean_values, 'seq', axis=0, tiled=True)]
    all_to_all x0 -> x1, starting transfers between devices: none -> 11.8 us  [lead_page(): y_new = lax.all_to_all(tile_out, 'fsdp', 0, 0)]
  transfers between devices with their start and end apart: 4 -> 4, of which waited for: 4 -> 3; matrix products, arithmetic and copies ran while one was open for 5% -> 6% of each run, Pallas kernels for 0% -> 0%
where the time goes in v1:
time: 382 us; the launch traced here: 381 us
  waiting for transfers between devices  221 us (58%)
  local copies, waits for them, and re-layouts  63.7 us (17%)
  matrix products  47.1 us (12%)
  other arithmetic  22.2 us (6%)
  between operations  13.3 us (3%)
  starting transfers between devices  12 us (3%)
    all_gather x1, waiting for transfers between devices, shards(): lax.all_gather(w_key, 'fsdp', axis=0, tiled=True)  143 us
    all_gather x1, waiting for transfers between devices, shards(): lax.all_gather(clean_values, 'seq', axis=0, tiled=True)  41.1 us
    all_gather x1, waiting for transfers between devices, shards(): lax.all_gather(clean_keys, 'seq', axis=0, tiled=True)  36.6 us
    dot_general x17, matrix products, absorb(): jnp.einsum('qkgt,tkd->qkgd', weights.astype(jnp.bfloat16), value_part.res...  24.7 us
    while x80, local copies, waits for them, and re-layouts  21.7 us
    dynamic_slice x32, local copies, waits for them, and re-layouts, sub_step(): value_part = lax.dynamic_slice_in_dim(value_stack, offset, BLOCK, 0)  17.7 us
    reduce_sum x17, other arithmetic, absorb(): row_sum = row_sum * rescale + jnp.sum(weights, -1)  17.4 us
    dynamic_slice x16, local copies, waits for them, and re-layouts, sub_step(): key_part = lax.dynamic_slice_in_dim(key_stack, offset, BLOCK, 0)  15.6 us
  transfers between devices with their start and end apart: 4, of which 3 were waited for; matrix products, arithmetic and copies ran while one was open for 6% of the time, Pallas kernels for 0%

profile of v1, /device:TPU:1, one launch (start us, length us, event | category | flops | bytes accessed | tf_op | source)
XLA Modules:
  0.0 380.8 jit_solution(10466287877192879846)
XLA Ops:
  7.3 3.3 stack.2
  10.6 11.8 %all-to-all-start = ((bf16[16,256,512]{2,1,0:T(8,128)(2,1)}), bf16[16,256,512]{2,1,0:T(8,128)(2,1)}, u32[]{:S(2)}, u32[]{:S(2)}) async-start(bf16[16,256,512]{2,1,0:T(8,128)(2,1)} %stack.2), calls=%async_computation | async-start | bytes 8388608 | tf_op jit(solution)/shard_map/all_to_all | solution.py:42
  23.5 142.8 %all-gather.4.cloned.1.call-done = bf16[4096,512]{1,0:T(8,128)(2,1)} async-done(((bf16[256,512]{1,0:T(8,128)(2,1)}), bf16[4096,512]{1,0:T(8,128)(2,1)}) %all-gather.4.cloned.1.call-update) | async-done | bytes 4194320 | tf_op jit(solution)/shard_map/all_gather | solution.py:46
  166.3 4.1 %fusion.34 = f32[257,512]{1,0:T(8,128)S(1)} fusion(bf16[4096,512]{1,0:T(8,128)(2,1)} %all-gather.4.cloned.1.call-done, bf16[1,4096]{1,0:T(2,128)(2,1)S(1)} %broadcast_in_dim.141, bf16[256,4096]{1,0:T(8,128)(2,1)} %bitcast.119), kind=kOutput, calls=%fused_computation.46 | convolution fusion | flops 1082146816 | bytes 6825984 | tf_op jit(solution)/shard_map/dot_general | solution.py:47
  173.1 4.2 %fusion.33 = f32[257,512]{1,0:T(8,128)S(1)} fusion(bf16[4096,512]{1,0:T(8,128)(2,1)} %bitcast.6, bf16[1,4096]{1,0:T(2,128)(2,1)S(1)} %broadcast_in_dim.141, bf16[256,4096]{1,0:T(8,128)(2,1)} %bitcast.120), kind=kOutput, calls=%fused_computation.45 | convolution fusion | flops 1082146816 | bytes 6825984 | tf_op jit(solution)/shard_map/dot_general | solution.py:48
  182.2 2.5 bitcast_add_fusion.1
  184.7 36.6 %all-gather.6.cloned.1.call-done = bf16[4096,512]{0,1:T(8,128)(2,1)} async-done(((bf16[256,512]{0,1:T(8,128)(2,1)}), bf16[4096,512]{0,1:T(8,128)(2,1)}) %all-gather.6.cloned.1.call-update) | async-done | bytes 4194320 | tf_op jit(solution)/shard_map/all_gather | solution.py:121
  221.3 41.1 %all-gather.8.cloned.1.call-done = bf16[4096,512]{1,0:T(8,128)(2,1)} async-done(((bf16[256,512]{1,0:T(8,128)(2,1)}), bf16[4096,512]{1,0:T(8,128)(2,1)}) %all-gather.8.cloned.1.call-update) | async-done | bytes 4194320 | tf_op jit(solution)/shard_map/all_gather | solution.py:122
  262.4 108.6 %while.13 = (s32[]{:T(128)}, f32[256,4,4]{0,2,1:T(4,128)S(1)}, f32[256,4,4]{0,2,1:T(4,128)S(1)}, f32[256,4,4,128]{0,3,2,1:T(8,128)}, bf16[4096,512]{0,1:T(8,128)...) while((s32[]{:T(128)}, f32[256,4,4]{0,2,1:T(4,128)S(1)}, ...), condition=%wide.region_5.6_spmd.clone, body=%wide.region_2.5_spmd.clone.sunk | while | flops 551563776 | bytes 36963736 | solution.py:112
  266.5 1.4 bitcast_add_fusion.3
  273.2 1.4 bitcast_add_fusion.3
  280.0 1.4 bitcast_add_fusion.3
  286.8 1.4 bitcast_add_fusion.3
  293.6 1.4 bitcast_add_fusion.3
  300.4 1.4 bitcast_add_fusion.3
  307.2 1.4 bitcast_add_fusion.3
  314.0 1.4 bitcast_add_fusion.3
  320.8 1.4 bitcast_add_fusion.3
  327.5 1.4 bitcast_add_fusion.3
  334.3 1.4 bitcast_add_fusion.3
  341.1 1.4 bitcast_add_fusion.3
  368.3 1.4 bitcast_add_fusion.3
  371.0 1.8 divide_convert_fusion
  372.8 1.4 copy.34
  (250 shorter events, 98.6 us)
Async XLA Ops:
  6.5 159.7 %all-gather.4.cloned.1.call-start = ((), (), s32[]{:S(2)}) async-start(), calls=%async_computation.1 | async-start | bytes 4456448 | tf_op jit(solution)/shard_map/all_gather | solution.py:46
  10.6 11.8 %copy-start.4 = (bf16[4096]{0:T(1024)(128)(2,1)S(1)}, bf16[4096]{0:T(1024)(128)(2,1)}, u32[]{:S(2)}) copy-start(bf16[4096]{0:T(1024)(128)(2,1)} %param.10) | copy-start | bytes 24580
  10.6 11.9 %copy-start.5 = (s32[1,256]{1,0:T(1,128)S(1)}, s32[1,256]{1,0:T(1,128)}, u32[]{:S(2)}) copy-start(s32[1,256]{1,0:T(1,128)} %param.9) | copy-start | bytes 3076
  10.6 162.5 %all-to-all-start = ((bf16[16,256,512]{2,1,0:T(8,128)(2,1)}), bf16[16,256,512]{2,1,0:T(8,128)(2,1)}, u32[]{:S(2)}, u32[]{:S(2)}) async-start(bf16[16,256,512]{2,1,0:T(8,128)(2,1)} %stack.2), calls=%async_computation | async-start | bytes 8388608 | tf_op jit(solution)/shard_map/all_to_all | solution.py:42
  22.3 198.9 %all-gather.6.cloned.1.call-start = ((), (), s32[]{:S(2)}) async-start(), calls=%async_computation.2 | async-start | bytes 4456448 | tf_op jit(solution)/shard_map/all_gather | solution.py:121
  172.9 89.6 %all-gather.8.cloned.1.call-start = ((), (), s32[]{:S(2)}) async-start(), calls=%async_computation.3 | async-start | bytes 4456448 | tf_op jit(solution)/shard_map/all_gather | solution.py:122
  173.1 5.0 %copy-start.2 = (bf16[1,256,2048]{2,1,0:T(8,128)(2,1)S(1)}, bf16[1,256,2048]{2,1,0:T(8,128)(2,1)}, u32[]{:S(2)}) copy-start(bf16[1,256,2048]{2,1,0:T(8,128)(2,1)} %param.11) | copy-start | bytes 3145732
  180.2 1.9 copy-start.3
  264.5 1.9 copy-start
  271.3 1.9 copy-start
  278.1 1.9 copy-start
  284.9 1.9 copy-start
  291.7 1.9 copy-start
  298.5 1.9 copy-start
  305.3 1.9 copy-start
  312.1 1.9 copy-start
  318.8 1.9 copy-start
  325.6 1.9 copy-start
  332.4 1.9 copy-start
  339.2 1.9 copy-start
  346.0 1.9 copy-start
  352.8 1.9 copy-start
  359.6 1.9 copy-start
  366.4 1.9 copy-start
  (16 other events, 21.9 us)
Sparse Core Ops, SparseCore 0:
  9.9 156.2 all-gather.3
  173.0 48.2 all-gather.5
  223.1 39.2 all-gather.7
